TPU v7x, 32 devices: a whole 2x2x4 slice. The times are simulated.
32 devices in a mesh: ens: 2 (over y), lat: 4 (over x, core), lon: 4 (over z).
Axes of the slice: x: 2, y: 2, z: 4, core: 2. Of those that a mesh axis runs over, the one named last changes fastest.
Arguments:
- state_now: float32 [6, 1152, 2304], P('ens', 'lat', 'lon'), parts along dimension 0, may hold values from -2 to 2, as said below
- state_old: float32 [6, 1152, 2304], P('ens', 'lat', 'lon'), parts along dimension 0, may hold values from -6 to 6
- polar_cutoff: int32 [576], replicated, may hold values from 1 to 1152, as said below
Outputs:
- state_new: float32 [6, 1152, 2304], P('ens', 'lat', 'lon'), parts along dimension 0
There are 2 independent parts, one for each index of `ens`. A program takes and returns all parts, laid end to end along the dimension named above; an argument that names none is the same for every part. Nothing has to cross between parts.
Inputs may be any that keep to these rules, and one draw needn't show every extreme that they name: `polar_cutoff`: every entry is at least 1 and at most 1152; the two rows next to 45 degrees keep all wavenumbers up to 1152. `state_now`: component 0 (depth) lies between 0.25 and 1.75.
All inputs are finite; a program needn't handle non-finite values.
Results may differ from a plain program's by a relative error of at most 0.00005.
Values sent between devices are 32-bit elements; how exact they have to be, the bound alone decides.
A program may use at most 64 MiB of HBM per device.

v0:
```python
import functools
import math

import jax
import jax.numpy as jnp
import numpy as np
from jax import lax
from jax.experimental import pallas as pl
from jax.experimental.pallas import tpu as pltpu
from jax.sharding import PartitionSpec as P

LANES = 128
SUB = 8
MESH = pl.DeviceIdType.MESH
step_scale = 0.2
coriolis = 2.0
gravity = 1.0
highest = lax.Precision.HIGHEST


def padded(value, sides, width, wrap):
    for axis, dim in sides:
        devices, length = (lax.axis_size(axis), value.shape[dim])
        up = [(i, (i + 1) % devices) for i in range(devices if wrap else devices - 1)]
        down = [(j, i) for i, j in up]
        last = lax.slice_in_dim(value, length - width, length, axis=dim)
        leading = lax.slice_in_dim(value, 0, width, axis=dim)
        before = lax.ppermute(last, axis, up)
        after = lax.ppermute(leading, axis, down)
        value = jnp.concatenate([before, value, after], axis=dim)
    return value


def latitude_terms(row_index, lat_total):
    distance = jnp.minimum(row_index + 0.5, lat_total - row_index - 0.5)
    cosine_lat = jnp.sin(math.pi * distance / lat_total)
    sine_lat = -jnp.cos(math.pi * (row_index + 0.5) / lat_total)
    return (cosine_lat, sine_lat)


def tendencies(lat_padded, lon_padded, cos_ext, sine_lat, lat_total, lon_total):
    cosine_lat = cos_ext[1:-1]
    zonal_scale = (lon_total / (4.0 * lat_total) / cosine_lat)[:, None]
    metric = math.pi / lat_total * sine_lat / cosine_lat
    depth_lon, east_lon, north_lon = (lon_padded[0], lon_padded[1], lon_padded[2])
    depth_lat, east_lat, north_lat = (lat_padded[0], lat_padded[1], lat_padded[2])
    east = east_lon[:, 1:-1]
    north = north_lon[:, 1:-1]

    def zonal_change(field):
        return zonal_scale * (field[:, 2:] - field[:, :-2])

    def northward_change(field):
        return 0.5 * (field[2:] - field[:-2])

    mass_flux = depth_lat * north_lat * cos_ext[:, None]
    tend_depth = (
        -zonal_change(depth_lon * east_lon) - northward_change(mass_flux) / cosine_lat[:, None]
    )
    turning = coriolis * sine_lat[:, None] + metric[:, None] * east
    tend_east = (
        -east * zonal_change(east_lon)
        - north * northward_change(east_lat)
        + turning * north
        - gravity * zonal_change(depth_lon)
    )
    tend_north = (
        -east * zonal_change(north_lon)
        - north * northward_change(north_lat)
        - turning * east
        - gravity * northward_change(depth_lat)
    )
    return jnp.stack([tend_depth, tend_east, tend_north])


def angle_table(first_count, second_count, period):
    first_idx = jnp.arange(first_count, dtype=jnp.int32)
    second_idx = jnp.arange(second_count, dtype=jnp.int32)
    turns = first_idx[:, None] * second_idx[None, :] % period
    phase = turns.astype(jnp.float32) * (2.0 * math.pi / period)
    return (jnp.cos(phase), jnp.sin(phase))


def low_pass(signal, cutoff):
    count, length = signal.shape
    first = 1
    probe = 1
    while probe * probe <= length:
        if length % probe == 0:
            first = probe
        probe = probe + 1
    second = length // first
    cos_first, sin_first = angle_table(first, first, first)
    cos_second, sin_second = angle_table(second, second, second)
    cos_twist, sin_twist = angle_table(first, second, length)
    grid = signal.reshape(count, first, second)
    part_re = jnp.einsum("cpq,pk->ckq", grid, cos_first, precision=highest)
    part_im = -jnp.einsum("cpq,pk->ckq", grid, sin_first, precision=highest)
    twist_re = part_re * cos_twist + part_im * sin_twist
    twist_im = part_im * cos_twist - part_re * sin_twist
    spec_re = jnp.einsum("ckq,qm->ckm", twist_re, cos_second, precision=highest) + jnp.einsum(
        "ckq,qm->ckm", twist_im, sin_second, precision=highest
    )
    spec_im = jnp.einsum("ckq,qm->ckm", twist_im, cos_second, precision=highest) - jnp.einsum(
        "ckq,qm->ckm", twist_re, sin_second, precision=highest
    )
    wave = (
        jnp.arange(first, dtype=jnp.int32)[:, None]
        + first * jnp.arange(second, dtype=jnp.int32)[None, :]
    )
    limit = cutoff[:, None, None]
    keep = ((wave[None] <= limit) | (wave[None] >= length - limit)).astype(jnp.float32) * (
        1.0 / length
    )
    spec_re = spec_re * keep
    spec_im = spec_im * keep
    back_re = jnp.einsum("ckm,mq->ckq", spec_re, cos_second, precision=highest) - jnp.einsum(
        "ckm,mq->ckq", spec_im, sin_second, precision=highest
    )
    back_im = jnp.einsum("ckm,mq->ckq", spec_im, cos_second, precision=highest) + jnp.einsum(
        "ckm,mq->ckq", spec_re, sin_second, precision=highest
    )
    turn_re = back_re * cos_twist - back_im * sin_twist
    turn_im = back_im * cos_twist + back_re * sin_twist
    result = jnp.einsum("ckq,kp->cpq", turn_re, cos_first, precision=highest) - jnp.einsum(
        "ckq,kp->cpq", turn_im, sin_first, precision=highest
    )
    return result.reshape(count, length)


def per_device(state_now, state_old, polar_cutoff):
    lat_rows = state_now.shape[1]
    lon_cols = state_now.shape[2]
    lat_count = lax.axis_size("lat")
    lon_count = lax.axis_size("lon")
    lat_total = lat_rows * lat_count
    lon_total = lon_cols * lon_count
    lat_place = lax.axis_index("lat")
    lat_padded = padded(state_now, (("lat", 1),), 1, False)
    lon_padded = padded(state_now, (("lon", 2),), 1, True)
    row_index = (lat_place * lat_rows + jnp.arange(-1, lat_rows + 1, dtype=jnp.int32)).astype(
        jnp.float32
    )
    cos_ext, sin_ext = latitude_terms(row_index, lat_total)
    forcing = tendencies(lat_padded, lon_padded, cos_ext, sin_ext[1:-1], lat_total, lon_total)
    groups = lat_count * lon_count
    share = lat_rows // groups
    member = lax.axis_index(("lat", "lon"))
    south_cut = lax.dynamic_slice_in_dim(polar_cutoff, member * share, share)
    north_cut = lax.dynamic_slice_in_dim(polar_cutoff, lat_rows + member * share, share)
    band_cut = jnp.concatenate([south_cut, north_cut])
    block = lax.all_to_all(forcing, ("lat", "lon"), split_axis=1, concat_axis=2, tiled=True)
    items = block.shape[0]
    wide = block.shape[2]
    south_rows = block[:, :, :lon_total]
    north_rows = block[:, :, wide - lon_total :]
    polar_rows = jnp.concatenate([south_rows, north_rows], axis=1)
    smooth = low_pass(polar_rows.reshape(items * 2 * share, lon_total), jnp.tile(band_cut, items))
    smooth = smooth.reshape(items, 2 * share, lon_total)
    rebuilt = jnp.concatenate(
        [smooth[:, :share], block[:, :, lon_total : wide - lon_total], smooth[:, share:]], axis=2
    )
    filtered = lax.all_to_all(rebuilt, ("lat", "lon"), split_axis=2, concat_axis=1, tiled=True)
    return state_old + step_scale * filtered


def spectral_tables(total):
    tiles = total // LANES
    half = tiles // 2
    q = np.arange(LANES)[:, None]
    m = np.arange(LANES)[None, :]
    forward = np.zeros((half, 2 * LANES, 2 * LANES))
    inverse = np.zeros((half, 2 * LANES, 2 * LANES))
    wave = np.zeros((half, 2 * LANES), np.int64)

    def angle(k):
        return 2.0 * np.pi * ((q * k) % total) / total

    mid = LANES // 2
    re_m = np.arange(mid + 1)[None, :]
    im_m = np.arange(1, mid)[None, :]
    weight = np.where((re_m == 0) | (re_m == mid), 1.0, 2.0) / total
    k_re, k_im = tiles * re_m, tiles * im_m
    forward[0, :LANES, : mid + 1] = np.cos(angle(k_re))
    forward[0, :LANES, mid + 1 : LANES] = -np.sin(angle(k_im))
    inverse[0, : mid + 1, :LANES] = (np.cos(angle(k_re)) * weight).T
    inverse[0, mid + 1 : LANES, :LANES] = (-np.sin(angle(k_im)) * 2.0 / total).T
    k_odd = half + tiles * np.arange(mid)[None, :]
    odd = np.concatenate([np.cos(angle(k_odd)), -np.sin(angle(k_odd))], axis=1)
    forward[0, LANES:, LANES:] = odd
    inverse[0, LANES:, LANES:] = odd.T * 2.0 / total
    wave[0] = np.concatenate([k_re[0], k_im[0], k_odd[0], k_odd[0]])
    for r in range(1, half):
        k = r + tiles * m
        c, s = np.cos(angle(k)), np.sin(angle(k))
        forward[r] = np.block([[c, -s], [s, c]])
        inverse[r] = forward[r].T * 2.0 / total
        wave[r] = np.concatenate([k[0], k[0]])
    wave = np.minimum(wave, total - wave)

    def split(a):
        a = a.astype(np.float32)
        hi = a.astype(jnp.bfloat16)
        lo = (a - hi.astype(np.float32)).astype(jnp.bfloat16)
        return np.stack([hi, lo])

    wave = np.broadcast_to(wave[:, None, :], (half, SUB, 2 * LANES)).astype(np.int32)
    return split(forward), split(inverse), np.ascontiguousarray(wave)


def geometry_table(lat_total, lon_total):
    j = np.arange(lat_total, dtype=np.float64)

    def cosine(row):
        return np.sin(np.pi * np.minimum(row + 0.5, lat_total - row - 0.5) / lat_total)

    c = cosine(j)
    s = -np.cos(np.pi * (j + 0.5) / lat_total)
    table = np.zeros((lat_total, LANES))
    table[:, 0] = lon_total / (4.0 * lat_total * c)
    table[:, 1] = 0.5 * cosine(j + 1) / c
    table[:, 2] = 0.5 * cosine(j - 1) / c
    table[:, 3] = coriolis * s
    table[:, 4] = np.pi / lat_total * s / c
    return table.astype(np.float32)


def forward_radix(tile, tiles):
    half = tiles // 2
    x = [tile(p) for p in range(tiles)]
    even = [None] * (half + 1)
    odd = [None] * (half + 1)
    even[0], even[half] = x[0], x[half]
    for p in range(1, half):
        even[p] = x[p] + x[tiles - p]
        odd[p] = x[p] - x[tiles - p]
    re, im = [None] * (half + 1), [None] * (half + 1)
    for r in range(half // 2 + 1):
        e = parity_sum([(even[p], math.cos(2 * math.pi * p * r / tiles)) for p in range(0, half + 1, 2)])
        o = parity_sum([(even[p], math.cos(2 * math.pi * p * r / tiles)) for p in range(1, half + 1, 2)])
        re[r] = e + o
        re[half - r] = e - o
        if 0 < r:
            es = parity_sum([(odd[p], math.sin(2 * math.pi * p * r / tiles)) for p in range(2, half, 2)])
            os = parity_sum([(odd[p], math.sin(2 * math.pi * p * r / tiles)) for p in range(1, half, 2)])
            im[r] = -(es + os)
            im[half - r] = es - os
    return re, im


def parity_sum(terms):
    total = None
    for value, factor in terms:
        if abs(factor - 1.0) < 1e-12:
            term = value
        elif abs(factor + 1.0) < 1e-12:
            term = -value
        elif abs(factor) < 1e-12:
            continue
        else:
            term = value * np.float32(factor)
        total = term if total is None else total + term
    return total if total is not None else jnp.zeros_like(terms[0][0])


def inverse_radix(re, im, tiles):
    half = tiles // 2
    x = [None] * tiles
    for p in range(half // 2 + 1):
        ce = parity_sum([(re[r], math.cos(2 * math.pi * p * r / tiles)) for r in range(0, half + 1, 2)])
        co = parity_sum([(re[r], math.cos(2 * math.pi * p * r / tiles)) for r in range(1, half + 1, 2)])
        if p == 0:
            x[0] = ce + co
            x[half] = ce - co
            continue
        se = parity_sum([(im[r], math.sin(2 * math.pi * p * r / tiles)) for r in range(2, half, 2)])
        so = parity_sum([(im[r], math.sin(2 * math.pi * p * r / tiles)) for r in range(1, half, 2)])
        c, s = ce + co, se + so
        x[p] = c - s
        x[tiles - p] = c + s
        c, s = ce - co, so - se
        x[half - p] = c - s
        x[half + p] = c + s
    return x


def split_dot(value, table, r):
    hi = value.astype(jnp.bfloat16)
    lo = (value - hi.astype(jnp.float32)).astype(jnp.bfloat16)
    big, small = table[0, r], table[1, r]
    out = jnp.dot(hi, big, preferred_element_type=jnp.float32)
    out = out + jnp.dot(lo, big, preferred_element_type=jnp.float32)
    return out + jnp.dot(hi, small, preferred_element_type=jnp.float32)


def step_kernel(
    lat_count, lon_count, chunk,
    x_hbm, geo_hbm, cut_ref, wave_ref, fwd_hbm, inv_hbm, out_ref,
    xp, geo, tend, recv, ret, full, spec, fwd, inv, col_send, col_recv,
    load_sem, table_sem, row_send_sem, row_recv_sem, col_send_sem, col_recv_sem,
    go_send, go_recv, back_send, back_recv, own_sem,
):
    rows, cols = out_ref.shape[1], out_ref.shape[2]
    share = rows // lon_count
    chunks = share // chunk
    groups = rows // SUB
    tiles = lon_count * cols // LANES
    half = tiles // 2
    lat = lax.axis_index("lat")
    lon = lax.axis_index("lon")
    west = lax.rem(lon + lon_count - 1, lon_count)
    east = lax.rem(lon + 1, lon_count)
    polar = jnp.logical_or(lat == 0, lat == lat_count - 1)
    has_south = lat > 0
    has_north = lat < lat_count - 1

    load = pltpu.make_async_copy(x_hbm, xp.at[:, pl.ds(SUB, rows), :], load_sem)
    load.start()
    geo_load = pltpu.make_async_copy(
        geo_hbm.at[pl.ds(pl.multiple_of(lat * rows, SUB), rows), :], geo, table_sem.at[0]
    )
    geo_load.start()
    fwd_load = pltpu.make_async_copy(fwd_hbm, fwd, table_sem.at[1])
    inv_load = pltpu.make_async_copy(inv_hbm, inv, table_sem.at[2])
    fwd_load.start()
    inv_load.start()

    barrier = pltpu.get_barrier_semaphore()
    for k in range(1, lon_count):
        pl.semaphore_signal(
            barrier, inc=1, device_id={"lon": lax.rem(lon + k, lon_count)}, device_id_type=MESH
        )

    @pl.when(has_south)
    def _():
        pl.semaphore_signal(barrier, inc=1, device_id={"lat": lat - 1}, device_id_type=MESH)

    @pl.when(has_north)
    def _():
        pl.semaphore_signal(barrier, inc=1, device_id={"lat": lat + 1}, device_id_type=MESH)

    pl.semaphore_wait(
        barrier, lon_count - 1 + has_south.astype(jnp.int32) + has_north.astype(jnp.int32)
    )

    def to_south():
        return pltpu.make_async_remote_copy(
            src_ref=x_hbm.at[:, pl.ds(0, SUB), :], dst_ref=xp.at[:, pl.ds(rows + SUB, SUB), :],
            send_sem=row_send_sem.at[0], recv_sem=row_recv_sem.at[0],
            device_id={"lat": lat - 1}, device_id_type=MESH,
        )

    def to_north():
        return pltpu.make_async_remote_copy(
            src_ref=x_hbm.at[:, pl.ds(rows - SUB, SUB), :], dst_ref=xp.at[:, pl.ds(0, SUB), :],
            send_sem=row_send_sem.at[1], recv_sem=row_recv_sem.at[1],
            device_id={"lat": lat + 1}, device_id_type=MESH,
        )

    @pl.when(has_south)
    def _():
        to_south().start()

    @pl.when(has_north)
    def _():
        to_north().start()

    zero_rows = jnp.zeros((3, SUB, cols), jnp.float32)

    @pl.when(jnp.logical_not(has_south))
    def _():
        xp[:, 0:SUB, :] = zero_rows

    @pl.when(jnp.logical_not(has_north))
    def _():
        xp[:, rows + SUB : rows + 2 * SUB, :] = zero_rows

    load.wait()
    lane = lax.broadcasted_iota(jnp.int32, (SUB, LANES), 1)

    packed = [jnp.zeros((SUB, LANES), jnp.float32) for _ in range(6)]
    for g in range(groups):
        here = lane == g
        for c in range(3):
            block = slice(SUB + g * SUB, 2 * SUB + g * SUB)
            packed[2 * c] = jnp.where(here, xp[c, block, 0:1], packed[2 * c])
            packed[2 * c + 1] = jnp.where(here, xp[c, block, cols - 1 : cols], packed[2 * c + 1])
    for c in range(3):
        col_send[0, c] = packed[2 * c]
        col_send[1, c] = packed[2 * c + 1]

    def column_copy(side, target):
        return pltpu.make_async_remote_copy(
            src_ref=col_send.at[side], dst_ref=col_recv.at[side],
            send_sem=col_send_sem.at[side], recv_sem=col_recv_sem.at[side],
            device_id={"lon": target}, device_id_type=MESH,
        )

    first_out = column_copy(0, west)
    last_out = column_copy(1, east)
    first_out.start()
    last_out.start()
    geo_load.wait()
    first_out.wait()
    last_out.wait()

    @pl.when(has_south)
    def _():
        to_south().wait_send()
        to_north().wait_recv()

    @pl.when(has_north)
    def _():
        to_north().wait_send()
        to_south().wait_recv()

    sub_idx = lax.broadcasted_iota(jnp.int32, (SUB, cols), 0)

    def tendency_group(g):
        start = pl.multiple_of(g * SUB, SUB)
        terms = geo[pl.ds(start, SUB), :]
        zonal, up, down, turn, metric = [terms[:, i : i + 1] for i in range(5)]
        cur, north, south, diff, east_of, west_of = [], [], [], [], [], []
        for c in range(3):
            before = xp[c, pl.ds(start, SUB), :]
            here = xp[c, pl.ds(pl.multiple_of(start + SUB, SUB), SUB), :]
            after = xp[c, pl.ds(pl.multiple_of(start + 2 * SUB, SUB), SUB), :]
            north.append(pltpu.roll(jnp.where(sub_idx == 0, after, here), SUB - 1, 0))
            south.append(pltpu.roll(jnp.where(sub_idx == SUB - 1, before, here), 1, 0))
            on = lane == g
            right = jnp.sum(jnp.where(on, col_recv[0, c], 0.0), axis=1, keepdims=True)
            left = jnp.sum(jnp.where(on, col_recv[1, c], 0.0), axis=1, keepdims=True)
            east_of.append(jnp.concatenate([here[:, 1:], right], axis=1))
            west_of.append(jnp.concatenate([left, here[:, :-1]], axis=1))
            cur.append(here)
        h, u, v = cur
        t_h = -zonal * (east_of[0] * east_of[1] - west_of[0] * west_of[1]) - (
            up * (north[0] * north[2]) - down * (south[0] * south[2])
        )
        turning = turn + metric * u
        zu = zonal * u
        hv = 0.5 * v
        t_u = (
            turning * v - zu * (east_of[1] - west_of[1]) - hv * (north[1] - south[1])
            - zonal * (east_of[0] - west_of[0])
        )
        t_v = (
            -turning * u - zu * (east_of[2] - west_of[2]) - hv * (north[2] - south[2])
            - 0.5 * (north[0] - south[0])
        )
        tend[0, pl.ds(start, SUB), :] = t_h
        tend[1, pl.ds(start, SUB), :] = t_u
        tend[2, pl.ds(start, SUB), :] = t_v

    def aligned(i):
        return pl.multiple_of(i, SUB)

    def go_copy(part, target, source):
        return pltpu.make_async_remote_copy(
            src_ref=tend.at[:, pl.ds(aligned(target * share + part * chunk), chunk), :],
            dst_ref=recv.at[source, :, pl.ds(aligned(part * chunk), chunk), :],
            send_sem=go_send.at[target, part], recv_sem=go_recv.at[source, part],
            device_id={"lon": target}, device_id_type=MESH,
        )

    def back_copy(part, target, source):
        return pltpu.make_async_remote_copy(
            src_ref=ret.at[target, :, pl.ds(aligned(part * chunk), chunk), :],
            dst_ref=out_ref.at[:, pl.ds(aligned(source * share + part * chunk), chunk), :],
            send_sem=back_send.at[target, part], recv_sem=back_recv.at[source, part],
            device_id={"lon": target}, device_id_type=MESH,
        )

    def own_go(part):
        return pltpu.make_async_copy(
            tend.at[:, pl.ds(aligned(lon * share + part * chunk), chunk), :],
            recv.at[lon, :, pl.ds(aligned(part * chunk), chunk), :],
            own_sem.at[0, part],
        )

    def own_back(part):
        return pltpu.make_async_copy(
            ret.at[lon, :, pl.ds(aligned(part * chunk), chunk), :],
            out_ref.at[:, pl.ds(aligned(lon * share + part * chunk), chunk), :],
            own_sem.at[1, part],
        )

    @pl.loop(0, chunks)
    def _(part):
        @pl.loop(1, lon_count + 1)
        def _(k):
            target = lax.rem(lon + k, lon_count)
            first = (target * share + part * chunk) // SUB

            @pl.loop(0, chunk // SUB)
            def _(i):
                tendency_group(first + i)

            @pl.when(jnp.logical_and(polar, k < lon_count))
            def _():
                go_copy(part, target, lon).start()

        @pl.when(polar)
        def _():
            own_go(part).start()

    fwd_load.wait()
    inv_load.wait()

    @pl.when(jnp.logical_not(polar))
    def _():
        keep = pltpu.make_async_copy(tend, out_ref, load_sem)
        keep.start()
        keep.wait()

    @pl.when(polar)
    def _():
        @pl.loop(0, chunks)
        def _(part):
            own_go(part).wait()
            for k in range(1, lon_count):
                source = lax.rem(lon + k, lon_count)
                go_copy(part, lon, source).wait_recv()
            at = pl.ds(aligned(part * chunk), chunk)
            for c in range(3):
                for d in range(lon_count):
                    full[c * chunk : (c + 1) * chunk, d * cols : (d + 1) * cols] = recv[d, c, at, :]

            @pl.loop(0, 3 * chunk // SUB)
            def _(g):
                block = pl.ds(aligned(g * SUB), SUB)
                re, im = forward_radix(lambda p: full[block, p * LANES : (p + 1) * LANES], tiles)
                spec[0, block, :LANES] = re[0]
                spec[0, block, LANES:] = re[half]
                for r in range(1, half):
                    spec[r, block, :LANES] = re[r]
                    spec[r, block, LANES:] = im[r]

            limit = cut_ref[at, :]
            limit = jnp.concatenate([limit, limit], axis=1)
            limit = jnp.concatenate([limit, limit, limit], axis=0)

            @pl.loop(0, half)
            def _(r):
                z = split_dot(spec[r], fwd, r)
                z = jnp.where(wave_ref[r, 0:1, :] <= limit, z, 0.0)
                spec[r] = split_dot(z, inv, r)

            @pl.loop(0, 3 * chunk // SUB)
            def _(g):
                block = pl.ds(aligned(g * SUB), SUB)
                re = [spec[r, block, :LANES] for r in range(half)] + [spec[0, block, LANES:]]
                im = [None] + [spec[r, block, LANES:] for r in range(1, half)]
                x = inverse_radix(re, im, tiles)
                for p in range(tiles):
                    full[block, p * LANES : (p + 1) * LANES] = x[p]

            for c in range(3):
                for d in range(lon_count):
                    ret[d, c, at, :] = full[c * chunk : (c + 1) * chunk, d * cols : (d + 1) * cols]
            own_back(part).start()
            for k in range(1, lon_count):
                back_copy(part, lax.rem(lon + k, lon_count), lon).start()

        @pl.loop(0, chunks)
        def _(part):
            own_back(part).wait()
            for k in range(1, lon_count):
                other = lax.rem(lon + k, lon_count)
                go_copy(part, other, lon).wait_send()
                back_copy(part, other, lon).wait_send()
                back_copy(part, lon, other).wait_recv()


def fused_step(mesh_shape, tables, state_now, state_old, polar_cutoff):
    lat_count, lon_count = mesh_shape
    comps, rows, cols = state_now.shape
    share = rows // lon_count
    total = lon_count * cols
    half = total // LANES // 2
    chunk = chunk_rows(share)
    chunks = share // chunk
    geo, fwd, inv, wave = tables
    lat = lax.axis_index("lat")
    lon = lax.axis_index("lon")
    start = jnp.where(lat == 0, 0, rows) + lon * share
    cut = lax.dynamic_slice_in_dim(polar_cutoff, start, share)
    cut = jnp.broadcast_to(cut[:, None], (share, LANES))
    any_spec = pl.BlockSpec(memory_space=pl.ANY)
    vmem_spec = pl.BlockSpec(memory_space=pltpu.VMEM)
    dma = pltpu.SemaphoreType.DMA
    filtered = pl.pallas_call(
        functools.partial(step_kernel, lat_count, lon_count, chunk),
        out_shape=jax.ShapeDtypeStruct(state_now.shape, jnp.float32),
        in_specs=[any_spec, any_spec, vmem_spec, vmem_spec, any_spec, any_spec],
        out_specs=vmem_spec,
        scratch_shapes=[
            pltpu.VMEM((comps, rows + 2 * SUB, cols), jnp.float32),
            pltpu.VMEM((rows, LANES), jnp.float32),
            pltpu.VMEM((comps, rows, cols), jnp.float32),
            pltpu.VMEM((lon_count, comps, share, cols), jnp.float32),
            pltpu.VMEM((lon_count, comps, share, cols), jnp.float32),
            pltpu.VMEM((comps * chunk, total), jnp.float32),
            pltpu.VMEM((half, comps * chunk, 2 * LANES), jnp.float32),
            pltpu.VMEM((2, half, 2 * LANES, 2 * LANES), jnp.bfloat16),
            pltpu.VMEM((2, half, 2 * LANES, 2 * LANES), jnp.bfloat16),
            pltpu.VMEM((2, comps, SUB, LANES), jnp.float32),
            pltpu.VMEM((2, comps, SUB, LANES), jnp.float32),
            dma, dma((3,)), dma((2,)), dma((2,)), dma((2,)), dma((2,)),
            dma((lon_count, chunks)), dma((lon_count, chunks)),
            dma((lon_count, chunks)), dma((lon_count, chunks)), dma((2, chunks)),
        ],
        compiler_params=pltpu.CompilerParams(
            collective_id=0, has_side_effects=True, vmem_limit_bytes=48 * 1024 * 1024
        ),
    )(state_now, geo, cut, wave, fwd, inv)
    return state_old + step_scale * filtered


def chunk_rows(share):
    for parts in (3, 2, 4, 1):
        if share % (parts * SUB) == 0:
            return share // parts
    return 0


def solution(mesh):
    lat_count, lon_count = mesh.shape["lat"], mesh.shape["lon"]

    def step(state_now, state_old, polar_cutoff):
        comps, lat_total, lon_total = state_now.shape
        rows, cols = lat_total // lat_count, lon_total // lon_count
        share = rows // lon_count
        fits = (
            lat_count >= 4 and lat_total == 4 * rows and rows % lon_count == 0
            and share % SUB == 0 and cols % (LANES // 2) == 0 and rows // SUB <= LANES
            and lon_total % (2 * LANES) == 0 and comps == 3 * mesh.shape["ens"]
        )
        body = per_device
        if fits:
            fwd, inv, wave = spectral_tables(lon_total)
            tables = (geometry_table(lat_total, lon_total), fwd, inv, wave)
            body = functools.partial(fused_step, (lat_count, lon_count), tables)
        return jax.shard_map(
            body,
            mesh=mesh,
            in_specs=(P("ens", "lat", "lon"), P("ens", "lat", "lon"), P()),
            out_specs=P("ens", "lat", "lon"),
            check_vma=False,
        )(state_now, state_old, polar_cutoff)

    return step
```

profile of v0, /device:TPU:0, one launch (start us, length us, event | category | flops | bytes accessed | tf_op | source)
XLA Modules:
  0.0 64.4 jit_solution(13974445191403535284)
XLA Ops:
  0.0 0.8 %dynamic_slice.3 = s32[72]{0:T(128)S(1)} dynamic-slice(s32[576]{0:T(1024)} %param.9, s32[]{:T(128)S(6)} %select_n.8), dynamic_slice_sizes={72} | dynamic-slice | bytes 580 | tf_op jit(solution)/shard_map/dynamic_slice | solution.py:587
  0.8 0.1 broadcast_in_dim.2.cut_ref
  0.8 0.0 copy-start
  0.8 1.6 %copy-done = f32[3,288,576]{2,1,0:T(8,128)S(1)} copy-done((f32[3,288,576]{2,1,0:T(8,128)S(1)}, f32[3,288,576]{2,1,0:T(8,128)}, u32[]{:S(2)}) %copy-start) | copy-done | bytes 1990680
  2.5 0.0 copy-start.1
  2.5 1.1 %copy-done.1 = f32[1152,128]{1,0:T(8,128)S(1)} copy-done((f32[1152,128]{1,0:T(8,128)S(1)}, f32[1152,128]{1,0:T(8,128)}, u32[]{:S(2)}) %copy-start.1) | copy-done | bytes 589848
  3.5 0.0 copy-start.2
  3.5 0.9 %copy-done.2 = s32[9,8,256]{2,1,0:T(8,128)S(1)} copy-done((s32[9,8,256]{2,1,0:T(8,128)S(1)}, s32[9,8,256]{2,1,0:T(8,128)}, u32[]{:S(2)}) %copy-start.2) | copy-done | bytes 73752
  4.4 0.0 copy-start.3
  4.4 58.4 %shard_map.73 = f32[3,288,576]{2,1,0:T(8,128)S(1)} custom-call(f32[3,288,576]{2,1,0:T(8,128)S(1)} %copy-done, f32[1152,128]{1,0:T(8,128)S(1)} %copy-done.1, s32[72,128]{1,0:T(8,128)S(1)} %broadcast_in_dim.2.cut_ref, s32[9,8,256]{2,1,0:T(8,128)S(1)} %copy-done.2, bf16[2,9,256,256]{3,2,1,0:T(8,128)(2,1)} %constant.27.clone.fwd_hbm, ...), custom_call_target="tpu_custom_call" | custom-call | tf_op jit(solution)/shard_map/pallas_call | solution.py:592
  62.8 0.0 copy-done.3
  62.8 1.6 %multiply_add_fusion = f32[3,288,576]{2,1,0:T(8,128)} fusion(f32[3,288,576]{2,1,0:T(8,128)S(1)} %copy-done.3, f32[3,288,576]{2,1,0:T(8,128)S(1)} %shard_map.73), kind=kLoop, calls=%fused_computation | loop fusion | flops 995328 | bytes 5971968 | tf_op jit(solution)/shard_map/add | solution.py:617
Async XLA Ops:
  0.8 1.6 %copy-start = (f32[3,288,576]{2,1,0:T(8,128)S(1)}, f32[3,288,576]{2,1,0:T(8,128)}, u32[]{:S(2)}) copy-start(f32[3,288,576]{2,1,0:T(8,128)} %x_hbm.1) | copy-start | bytes 5971972
  2.5 1.1 %copy-start.1 = (f32[1152,128]{1,0:T(8,128)S(1)}, f32[1152,128]{1,0:T(8,128)}, u32[]{:S(2)}) copy-start(f32[1152,128]{1,0:T(8,128)} %constant.25.clone.geo_hbm) | copy-start | bytes 1769476
  3.5 0.9 %copy-start.2 = (s32[9,8,256]{2,1,0:T(8,128)S(1)}, s32[9,8,256]{2,1,0:T(8,128)}, u32[]{:S(2)}) copy-start(s32[9,8,256]{2,1,0:T(8,128)} %constant.26.clone.wave_ref) | copy-start | bytes 221188
  4.4 58.4 %copy-start.3 = (f32[3,288,576]{2,1,0:T(8,128)S(1)}, f32[3,288,576]{2,1,0:T(8,128)}, u32[]{:S(2)}) copy-start(f32[3,288,576]{2,1,0:T(8,128)} %param.8) | copy-start | bytes 5971972
where the time goes:
time: 64.7 us; the launch traced here: 64.4 us
  Pallas kernels  58.4 us (90%)
  local copies, waits for them, and re-layouts  4.41 us (7%)
  other arithmetic  1.6 us (2%)
    pallas_call x1, Pallas kernels, fused_step(): pl.pallas_call(functools.partial(step_kernel, lat_count, lon_count, chunk...  58.4 us
    unnamed x8, local copies, waits for them, and re-layouts  3.58 us
    add x1, other arithmetic, fused_step(): return state_old + step_scale * filtered  1.6 us

commit v1 on v0

--- a/solution.py
+++ b/solution.py
@@ -170,7 +170,6 @@
     q = np.arange(LANES)[:, None]
     m = np.arange(LANES)[None, :]
     forward = np.zeros((half, 2 * LANES, 2 * LANES))
-    inverse = np.zeros((half, 2 * LANES, 2 * LANES))
     wave = np.zeros((half, 2 * LANES), np.int64)
 
     def angle(k):
@@ -179,22 +178,17 @@
     mid = LANES // 2
     re_m = np.arange(mid + 1)[None, :]
     im_m = np.arange(1, mid)[None, :]
-    weight = np.where((re_m == 0) | (re_m == mid), 1.0, 2.0) / total
     k_re, k_im = tiles * re_m, tiles * im_m
     forward[0, :LANES, : mid + 1] = np.cos(angle(k_re))
     forward[0, :LANES, mid + 1 : LANES] = -np.sin(angle(k_im))
-    inverse[0, : mid + 1, :LANES] = (np.cos(angle(k_re)) * weight).T
-    inverse[0, mid + 1 : LANES, :LANES] = (-np.sin(angle(k_im)) * 2.0 / total).T
     k_odd = half + tiles * np.arange(mid)[None, :]
     odd = np.concatenate([np.cos(angle(k_odd)), -np.sin(angle(k_odd))], axis=1)
     forward[0, LANES:, LANES:] = odd
-    inverse[0, LANES:, LANES:] = odd.T * 2.0 / total
     wave[0] = np.concatenate([k_re[0], k_im[0], k_odd[0], k_odd[0]])
     for r in range(1, half):
         k = r + tiles * m
         c, s = np.cos(angle(k)), np.sin(angle(k))
         forward[r] = np.block([[c, -s], [s, c]])
-        inverse[r] = forward[r].T * 2.0 / total
         wave[r] = np.concatenate([k[0], k[0]])
     wave = np.minimum(wave, total - wave)
 
@@ -204,8 +198,11 @@
         lo = (a - hi.astype(np.float32)).astype(jnp.bfloat16)
         return np.stack([hi, lo])
 
-    wave = np.broadcast_to(wave[:, None, :], (half, SUB, 2 * LANES)).astype(np.int32)
-    return split(forward), split(inverse), np.ascontiguousarray(wave)
+    bins = np.zeros((half, SUB, 2 * LANES), np.float32)
+    bins[:, 0] = wave
+    bins[:, 1] = 2.0 / total
+    bins[0, 1, [0, mid]] = 1.0 / total
+    return split(forward), bins
 
 
 def geometry_table(lat_total, lon_total):
@@ -284,21 +281,24 @@
     return x
 
 
-def split_dot(value, table, r):
+def split_dot(value, table, r, transpose):
     hi = value.astype(jnp.bfloat16)
     lo = (value - hi.astype(jnp.float32)).astype(jnp.bfloat16)
     big, small = table[0, r], table[1, r]
-    out = jnp.dot(hi, big, preferred_element_type=jnp.float32)
-    out = out + jnp.dot(lo, big, preferred_element_type=jnp.float32)
-    return out + jnp.dot(hi, small, preferred_element_type=jnp.float32)
+    dims = (((1,), (1 if transpose else 0,)), ((), ()))
+
+    def dot(a, b):
+        return lax.dot_general(a, b, dims, preferred_element_type=jnp.float32)
+
+    return dot(hi, big) + dot(lo, big) + dot(hi, small)
 
 
 def step_kernel(
     lat_count, lon_count, chunk,
-    x_hbm, geo_hbm, cut_ref, wave_ref, fwd_hbm, inv_hbm, out_ref,
-    xp, geo, tend, recv, ret, full, spec, fwd, inv, col_send, col_recv,
+    x_hbm, geo_hbm, cut_hbm, bins_hbm, fwd_hbm, out_ref,
+    xp, geo, cut_ref, bins, go, recv, ret, back, full, spec, fwd, col_send, col_recv,
     load_sem, table_sem, row_send_sem, row_recv_sem, col_send_sem, col_recv_sem,
-    go_send, go_recv, back_send, back_recv, own_sem,
+    go_send, go_recv, back_send, back_recv,
 ):
     rows, cols = out_ref.shape[1], out_ref.shape[2]
     share = rows // lon_count
@@ -320,10 +320,12 @@
         geo_hbm.at[pl.ds(pl.multiple_of(lat * rows, SUB), rows), :], geo, table_sem.at[0]
     )
     geo_load.start()
-    fwd_load = pltpu.make_async_copy(fwd_hbm, fwd, table_sem.at[1])
-    inv_load = pltpu.make_async_copy(inv_hbm, inv, table_sem.at[2])
-    fwd_load.start()
-    inv_load.start()
+    table_loads = [
+        pltpu.make_async_copy(src, dst, table_sem.at[i + 1])
+        for i, (src, dst) in enumerate([(fwd_hbm, fwd), (bins_hbm, bins), (cut_hbm, cut_ref)])
+    ]
+    for copy in table_loads:
+        copy.start()
 
     barrier = pltpu.get_barrier_semaphore()
     for k in range(1, lon_count):
@@ -338,42 +340,6 @@
     @pl.when(has_north)
     def _():
         pl.semaphore_signal(barrier, inc=1, device_id={"lat": lat + 1}, device_id_type=MESH)
-
-    pl.semaphore_wait(
-        barrier, lon_count - 1 + has_south.astype(jnp.int32) + has_north.astype(jnp.int32)
-    )
-
-    def to_south():
-        return pltpu.make_async_remote_copy(
-            src_ref=x_hbm.at[:, pl.ds(0, SUB), :], dst_ref=xp.at[:, pl.ds(rows + SUB, SUB), :],
-            send_sem=row_send_sem.at[0], recv_sem=row_recv_sem.at[0],
-            device_id={"lat": lat - 1}, device_id_type=MESH,
-        )
-
-    def to_north():
-        return pltpu.make_async_remote_copy(
-            src_ref=x_hbm.at[:, pl.ds(rows - SUB, SUB), :], dst_ref=xp.at[:, pl.ds(0, SUB), :],
-            send_sem=row_send_sem.at[1], recv_sem=row_recv_sem.at[1],
-            device_id={"lat": lat + 1}, device_id_type=MESH,
-        )
-
-    @pl.when(has_south)
-    def _():
-        to_south().start()
-
-    @pl.when(has_north)
-    def _():
-        to_north().start()
-
-    zero_rows = jnp.zeros((3, SUB, cols), jnp.float32)
-
-    @pl.when(jnp.logical_not(has_south))
-    def _():
-        xp[:, 0:SUB, :] = zero_rows
-
-    @pl.when(jnp.logical_not(has_north))
-    def _():
-        xp[:, rows + SUB : rows + 2 * SUB, :] = zero_rows
 
     load.wait()
     lane = lax.broadcasted_iota(jnp.int32, (SUB, LANES), 1)
@@ -388,6 +354,42 @@
     for c in range(3):
         col_send[0, c] = packed[2 * c]
         col_send[1, c] = packed[2 * c + 1]
+
+    pl.semaphore_wait(
+        barrier, lon_count - 1 + has_south.astype(jnp.int32) + has_north.astype(jnp.int32)
+    )
+
+    def to_south():
+        return pltpu.make_async_remote_copy(
+            src_ref=x_hbm.at[:, pl.ds(0, SUB), :], dst_ref=xp.at[:, pl.ds(rows + SUB, SUB), :],
+            send_sem=row_send_sem.at[0], recv_sem=row_recv_sem.at[0],
+            device_id={"lat": lat - 1}, device_id_type=MESH,
+        )
+
+    def to_north():
+        return pltpu.make_async_remote_copy(
+            src_ref=x_hbm.at[:, pl.ds(rows - SUB, SUB), :], dst_ref=xp.at[:, pl.ds(0, SUB), :],
+            send_sem=row_send_sem.at[1], recv_sem=row_recv_sem.at[1],
+            device_id={"lat": lat + 1}, device_id_type=MESH,
+        )
+
+    @pl.when(has_south)
+    def _():
+        to_south().start()
+
+    @pl.when(has_north)
+    def _():
+        to_north().start()
+
+    zero_rows = jnp.zeros((3, SUB, cols), jnp.float32)
+
+    @pl.when(jnp.logical_not(has_south))
+    def _():
+        xp[:, 0:SUB, :] = zero_rows
+
+    @pl.when(jnp.logical_not(has_north))
+    def _():
+        xp[:, rows + SUB : rows + 2 * SUB, :] = zero_rows
 
     def column_copy(side, target):
         return pltpu.make_async_remote_copy(
@@ -448,83 +450,100 @@
             -turning * u - zu * (east_of[2] - west_of[2]) - hv * (north[2] - south[2])
             - 0.5 * (north[0] - south[0])
         )
-        tend[0, pl.ds(start, SUB), :] = t_h
-        tend[1, pl.ds(start, SUB), :] = t_u
-        tend[2, pl.ds(start, SUB), :] = t_v
+        return t_h, t_u, t_v
 
     def aligned(i):
         return pl.multiple_of(i, SUB)
 
+    per_chunk = chunk // SUB
+    whole = cols // LANES
+    half_at = whole * 3 * chunk
+
+    def half_place(group):
+        return pl.ds(half_at + group // 2 * SUB, SUB), pl.ds(group % 2 * (LANES // 2), LANES // 2)
+
     def go_copy(part, target, source):
         return pltpu.make_async_remote_copy(
-            src_ref=tend.at[:, pl.ds(aligned(target * share + part * chunk), chunk), :],
-            dst_ref=recv.at[source, :, pl.ds(aligned(part * chunk), chunk), :],
+            src_ref=go.at[target, part], dst_ref=recv.at[source, part],
             send_sem=go_send.at[target, part], recv_sem=go_recv.at[source, part],
             device_id={"lon": target}, device_id_type=MESH,
         )
 
     def back_copy(part, target, source):
         return pltpu.make_async_remote_copy(
-            src_ref=ret.at[target, :, pl.ds(aligned(part * chunk), chunk), :],
-            dst_ref=out_ref.at[:, pl.ds(aligned(source * share + part * chunk), chunk), :],
+            src_ref=ret.at[target, part], dst_ref=back.at[source, part],
             send_sem=back_send.at[target, part], recv_sem=back_recv.at[source, part],
             device_id={"lon": target}, device_id_type=MESH,
         )
 
-    def own_go(part):
-        return pltpu.make_async_copy(
-            tend.at[:, pl.ds(aligned(lon * share + part * chunk), chunk), :],
-            recv.at[lon, :, pl.ds(aligned(part * chunk), chunk), :],
-            own_sem.at[0, part],
-        )
-
-    def own_back(part):
-        return pltpu.make_async_copy(
-            ret.at[lon, :, pl.ds(aligned(part * chunk), chunk), :],
-            out_ref.at[:, pl.ds(aligned(lon * share + part * chunk), chunk), :],
-            own_sem.at[1, part],
-        )
-
-    @pl.loop(0, chunks)
-    def _(part):
-        @pl.loop(1, lon_count + 1)
-        def _(k):
-            target = lax.rem(lon + k, lon_count)
-            first = (target * share + part * chunk) // SUB
-
-            @pl.loop(0, chunk // SUB)
-            def _(i):
-                tendency_group(first + i)
-
-            @pl.when(jnp.logical_and(polar, k < lon_count))
-            def _():
-                go_copy(part, target, lon).start()
-
-        @pl.when(polar)
-        def _():
-            own_go(part).start()
-
-    fwd_load.wait()
-    inv_load.wait()
-
-    @pl.when(jnp.logical_not(polar))
-    def _():
-        keep = pltpu.make_async_copy(tend, out_ref, load_sem)
-        keep.start()
-        keep.wait()
+    def make_piece(buf, place, part, target):
+        first = (target * share + part * chunk) // SUB
+        for i in range(per_chunk):
+            values = tendency_group(first + i)
+            for c in range(3):
+                group = c * per_chunk + i
+                for t in range(whole):
+                    buf[place, part, t * 3 * chunk + group * SUB : t * 3 * chunk + (group + 1) * SUB, :] = (
+                        values[c][:, t * LANES : (t + 1) * LANES]
+                    )
+                if cols % LANES:
+                    at_rows, at_lanes = half_place(group)
+                    buf[place, part, at_rows, at_lanes] = values[c][:, whole * LANES :]
+
+    def unpack(buf, part, source):
+        first = source * share + part * chunk
+        for c in range(3):
+            for t in range(whole):
+                out_ref[c, pl.ds(aligned(first), chunk), t * LANES : (t + 1) * LANES] = buf[
+                    source, part, pl.ds((t * 3 + c) * chunk, chunk), :
+                ]
+            if cols % LANES:
+                for i in range(per_chunk):
+                    at_rows, at_lanes = half_place(c * per_chunk + i)
+                    out_ref[c, pl.ds(aligned(first + i * SUB), SUB), whole * LANES :] = buf[
+                        source, part, at_rows, at_lanes
+                    ]
 
     @pl.when(polar)
     def _():
         @pl.loop(0, chunks)
         def _(part):
-            own_go(part).wait()
+            @pl.loop(1, lon_count)
+            def _(k):
+                target = lax.rem(lon + k, lon_count)
+                make_piece(go, target, part, target)
+                go_copy(part, target, lon).start()
+
+            make_piece(recv, lon, part, lon)
+
+    @pl.when(jnp.logical_not(polar))
+    def _():
+        @pl.loop(0, groups)
+        def _(g):
+            values = tendency_group(g)
+            for c in range(3):
+                out_ref[c, pl.ds(aligned(g * SUB), SUB), :] = values[c]
+
+    for copy in table_loads:
+        copy.wait()
+
+    cut_start = jnp.where(lat == 0, 0, rows) + lon * share
+
+    @pl.when(polar)
+    def _():
+        @pl.loop(0, chunks)
+        def _(part):
             for k in range(1, lon_count):
-                source = lax.rem(lon + k, lon_count)
-                go_copy(part, lon, source).wait_recv()
-            at = pl.ds(aligned(part * chunk), chunk)
-            for c in range(3):
-                for d in range(lon_count):
-                    full[c * chunk : (c + 1) * chunk, d * cols : (d + 1) * cols] = recv[d, c, at, :]
+                go_copy(part, lon, lax.rem(lon + k, lon_count)).wait_recv()
+            for d in range(lon_count):
+                for t in range(whole):
+                    lanes = slice(d * cols + t * LANES, d * cols + (t + 1) * LANES)
+                    full[:, lanes] = recv[d, part, t * 3 * chunk : (t + 1) * 3 * chunk, :]
+                if cols % LANES:
+                    lanes = slice(d * cols + whole * LANES, (d + 1) * cols)
+                    for group in range(3 * per_chunk):
+                        at_rows, at_lanes = half_place(group)
+                        full[group * SUB : (group + 1) * SUB, lanes] = recv[d, part, at_rows, at_lanes]
 
             @pl.loop(0, 3 * chunk // SUB)
             def _(g):
@@ -536,15 +555,17 @@
                     spec[r, block, :LANES] = re[r]
                     spec[r, block, LANES:] = im[r]
 
-            limit = cut_ref[at, :]
-            limit = jnp.concatenate([limit, limit], axis=1)
+            wanted = cut_start + part * chunk + lax.broadcasted_iota(jnp.int32, (chunk, 2 * rows), 0)
+            hit = wanted == lax.broadcasted_iota(jnp.int32, (chunk, 2 * rows), 1)
+            cuts = cut_ref[0:1, :].astype(jnp.float32)
+            limit = jnp.sum(jnp.where(hit, cuts, 0.0), axis=1, keepdims=True)
             limit = jnp.concatenate([limit, limit, limit], axis=0)
 
             @pl.loop(0, half)
             def _(r):
-                z = split_dot(spec[r], fwd, r)
-                z = jnp.where(wave_ref[r, 0:1, :] <= limit, z, 0.0)
-                spec[r] = split_dot(z, inv, r)
+                z = split_dot(spec[r], fwd, r, False)
+                z = jnp.where(bins[r, 0:1, :] <= limit, z * bins[r, 1:2, :], 0.0)
+                spec[r] = split_dot(z, fwd, r, True)
 
             @pl.loop(0, 3 * chunk // SUB)
             def _(g):
@@ -555,21 +576,28 @@
                 for p in range(tiles):
                     full[block, p * LANES : (p + 1) * LANES] = x[p]
 
-            for c in range(3):
-                for d in range(lon_count):
-                    ret[d, c, at, :] = full[c * chunk : (c + 1) * chunk, d * cols : (d + 1) * cols]
-            own_back(part).start()
+            for d in range(lon_count):
+                for t in range(whole):
+                    lanes = slice(d * cols + t * LANES, d * cols + (t + 1) * LANES)
+                    ret[d, part, t * 3 * chunk : (t + 1) * 3 * chunk, :] = full[:, lanes]
+                if cols % LANES:
+                    lanes = slice(d * cols + whole * LANES, (d + 1) * cols)
+                    for group in range(3 * per_chunk):
+                        at_rows, at_lanes = half_place(group)
+                        ret[d, part, at_rows, at_lanes] = full[group * SUB : (group + 1) * SUB, lanes]
             for k in range(1, lon_count):
                 back_copy(part, lax.rem(lon + k, lon_count), lon).start()
+            unpack(ret, part, lon)
 
         @pl.loop(0, chunks)
         def _(part):
-            own_back(part).wait()
-            for k in range(1, lon_count):
+            @pl.loop(1, lon_count)
+            def _(k):
                 other = lax.rem(lon + k, lon_count)
                 go_copy(part, other, lon).wait_send()
+                back_copy(part, lon, other).wait_recv()
+                unpack(back, part, other)
                 back_copy(part, other, lon).wait_send()
-                back_copy(part, lon, other).wait_recv()
 
 
 def fused_step(mesh_shape, tables, state_now, state_old, polar_cutoff):
@@ -580,40 +608,43 @@
     half = total // LANES // 2
     chunk = chunk_rows(share)
     chunks = share // chunk
-    geo, fwd, inv, wave = tables
-    lat = lax.axis_index("lat")
-    lon = lax.axis_index("lon")
-    start = jnp.where(lat == 0, 0, rows) + lon * share
-    cut = lax.dynamic_slice_in_dim(polar_cutoff, start, share)
-    cut = jnp.broadcast_to(cut[:, None], (share, LANES))
-    any_spec = pl.BlockSpec(memory_space=pl.ANY)
+    geo, fwd, bins = tables
+    groups = comps * chunk // SUB
+    piece = (cols // LANES * groups + (groups + 1) // 2 * (cols % LANES > 0)) * SUB
+    operands = [
+        pltpu.with_memory_space_constraint(jnp.asarray(a), pltpu.HBM)
+        for a in (state_now, geo, polar_cutoff.reshape(1, 2 * rows), bins, fwd)
+    ]
+    hbm_spec = pl.BlockSpec(memory_space=pltpu.HBM)
     vmem_spec = pl.BlockSpec(memory_space=pltpu.VMEM)
     dma = pltpu.SemaphoreType.DMA
     filtered = pl.pallas_call(
         functools.partial(step_kernel, lat_count, lon_count, chunk),
         out_shape=jax.ShapeDtypeStruct(state_now.shape, jnp.float32),
-        in_specs=[any_spec, any_spec, vmem_spec, vmem_spec, any_spec, any_spec],
+        in_specs=[hbm_spec] * 5,
         out_specs=vmem_spec,
         scratch_shapes=[
             pltpu.VMEM((comps, rows + 2 * SUB, cols), jnp.float32),
             pltpu.VMEM((rows, LANES), jnp.float32),
-            pltpu.VMEM((comps, rows, cols), jnp.float32),
-            pltpu.VMEM((lon_count, comps, share, cols), jnp.float32),
-            pltpu.VMEM((lon_count, comps, share, cols), jnp.float32),
+            pltpu.VMEM((1, 2 * rows), jnp.int32),
+            pltpu.VMEM((half, SUB, 2 * LANES), jnp.float32),
+            pltpu.VMEM((lon_count, chunks, piece, LANES), jnp.float32),
+            pltpu.VMEM((lon_count, chunks, piece, LANES), jnp.float32),
+            pltpu.VMEM((lon_count, chunks, piece, LANES), jnp.float32),
+            pltpu.VMEM((lon_count, chunks, piece, LANES), jnp.float32),
             pltpu.VMEM((comps * chunk, total), jnp.float32),
             pltpu.VMEM((half, comps * chunk, 2 * LANES), jnp.float32),
             pltpu.VMEM((2, half, 2 * LANES, 2 * LANES), jnp.bfloat16),
-            pltpu.VMEM((2, half, 2 * LANES, 2 * LANES), jnp.bfloat16),
             pltpu.VMEM((2, comps, SUB, LANES), jnp.float32),
             pltpu.VMEM((2, comps, SUB, LANES), jnp.float32),
-            dma, dma((3,)), dma((2,)), dma((2,)), dma((2,)), dma((2,)),
+            dma, dma((4,)), dma((2,)), dma((2,)), dma((2,)), dma((2,)),
             dma((lon_count, chunks)), dma((lon_count, chunks)),
-            dma((lon_count, chunks)), dma((lon_count, chunks)), dma((2, chunks)),
+            dma((lon_count, chunks)), dma((lon_count, chunks)),
         ],
         compiler_params=pltpu.CompilerParams(
             collective_id=0, has_side_effects=True, vmem_limit_bytes=48 * 1024 * 1024
         ),
-    )(state_now, geo, cut, wave, fwd, inv)
+    )(*operands)
     return state_old + step_scale * filtered
 
 
@@ -638,8 +669,7 @@
         )
         body = per_device
         if fits:
-            fwd, inv, wave = spectral_tables(lon_total)
-            tables = (geometry_table(lat_total, lon_total), fwd, inv, wave)
+            tables = (geometry_table(lat_total, lon_total), *spectral_tables(lon_total))
             body = functools.partial(fused_step, (lat_count, lon_count), tables)
         return jax.shard_map(
             body,

time: 64.7 us -> 58 us (0.90)
  Pallas kernels: 58.4 us -> 55 us
  local copies, waits for them, and re-layouts: 4.41 us -> 1.27 us
    unnamed x8 -> x2, local copies, waits for them, and re-layouts: 3.58 us -> 0.01 us
    pallas_call x1, Pallas kernels: 58.4 us -> 55 us  [fused_step(): pl.pallas_call(functools.partial(step_kernel, lat_count, lon_count, chunk...]
    reshape x0 -> x1, local copies, waits for them, and re-layouts: none -> 1.27 us  [fused_step(): polar_cutoff.reshape(1, 2 * rows)]
    dynamic_slice x1 -> x0, local copies, waits for them, and re-layouts: 0.76 us -> none  [fused_step(): cut = lax.dynamic_slice_in_dim(polar_cutoff, start, share)]
where the time goes in v1:
time: 58 us; the launch traced here: 57.8 us
  Pallas kernels  55 us (95%)
  other arithmetic  1.6 us (3%)
  local copies, waits for them, and re-layouts  1.27 us (2%)
    pallas_call x1, Pallas kernels, fused_step(): pl.pallas_call(functools.partial(step_kernel, lat_count, lon_count, chunk...  55 us
    add x1, other arithmetic, fused_step(): return state_old + step_scale * filtered  1.6 us
    reshape x1, local copies, waits for them, and re-layouts, fused_step(): polar_cutoff.reshape(1, 2 * rows)  1.27 us

profile of v1, /device:TPU:0, one launch (start us, length us, event | category | flops | bytes accessed | tf_op | source)
XLA Modules:
  0.0 57.8 jit_solution(1820033912757304692)
XLA Ops:
  0.0 1.3 %reshape.3.cut_hbm = s32[1,576]{1,0:T(1,128)} reshape(s32[576]{0:T(1024)} %param.8) | data formatting | bytes 4608 | tf_op jit(solution)/shard_map/reshape | solution.py:616
  1.3 0.0 copy-start
  1.3 55.0 %shard_map.64 = f32[3,288,576]{2,1,0:T(8,128)S(1)} custom-call(f32[3,288,576]{2,1,0:T(8,128)} %x_hbm.1, f32[1152,128]{1,0:T(8,128)} %constant.8.clone.geo_hbm, s32[1,576]{1,0:T(1,128)} %reshape.3.cut_hbm, f32[9,8,256]{2,1,0:T(8,128)} %constant.9.clone.bins_hbm, bf16[2,9,256,256]{3,2,1,0:T(8,128)(2,1)} %constant.10.clone.fwd_hbm), custom_call_target="tpu_custom_call" | custom-call | tf_op jit(solution)/shard_map/pallas_call | solution.py:621
  56.2 0.0 copy-done
  56.2 1.6 %multiply_add_fusion = f32[3,288,576]{2,1,0:T(8,128)} fusion(f32[3,288,576]{2,1,0:T(8,128)S(1)} %copy-done, f32[3,288,576]{2,1,0:T(8,128)S(1)} %shard_map.64), kind=kLoop, calls=%fused_computation | loop fusion | flops 995328 | bytes 5971968 | tf_op jit(solution)/shard_map/add | solution.py:648
Async XLA Ops:
  1.3 55.0 %copy-start = (f32[3,288,576]{2,1,0:T(8,128)S(1)}, f32[3,288,576]{2,1,0:T(8,128)}, u32[]{:S(2)}) copy-start(f32[3,288,576]{2,1,0:T(8,128)} %param.7) | copy-start | bytes 5971972

commit v2 on v1

--- a/solution.py
+++ b/solution.py
@@ -403,22 +403,9 @@
     first_out.start()
     last_out.start()
     geo_load.wait()
-    first_out.wait()
-    last_out.wait()
-
-    @pl.when(has_south)
-    def _():
-        to_south().wait_send()
-        to_north().wait_recv()
-
-    @pl.when(has_north)
-    def _():
-        to_north().wait_send()
-        to_south().wait_recv()
-
     sub_idx = lax.broadcasted_iota(jnp.int32, (SUB, cols), 0)
 
-    def tendency_group(g):
+    def tendency_group(g, edges=True):
         start = pl.multiple_of(g * SUB, SUB)
         terms = geo[pl.ds(start, SUB), :]
         zonal, up, down, turn, metric = [terms[:, i : i + 1] for i in range(5)]
@@ -429,9 +416,12 @@
             after = xp[c, pl.ds(pl.multiple_of(start + 2 * SUB, SUB), SUB), :]
             north.append(pltpu.roll(jnp.where(sub_idx == 0, after, here), SUB - 1, 0))
             south.append(pltpu.roll(jnp.where(sub_idx == SUB - 1, before, here), 1, 0))
-            on = lane == g
-            right = jnp.sum(jnp.where(on, col_recv[0, c], 0.0), axis=1, keepdims=True)
-            left = jnp.sum(jnp.where(on, col_recv[1, c], 0.0), axis=1, keepdims=True)
+            if edges:
+                on = lane == g
+                right = jnp.sum(jnp.where(on, col_recv[0, c], 0.0), axis=1, keepdims=True)
+                left = jnp.sum(jnp.where(on, col_recv[1, c], 0.0), axis=1, keepdims=True)
+            else:
+                right, left = here[:, -1:], here[:, :1]
             east_of.append(jnp.concatenate([here[:, 1:], right], axis=1))
             west_of.append(jnp.concatenate([left, here[:, :-1]], axis=1))
             cur.append(here)
@@ -452,6 +442,20 @@
         )
         return t_h, t_u, t_v
 
+    def halos_arrive():
+        first_out.wait()
+        last_out.wait()
+
+        @pl.when(has_south)
+        def _():
+            to_south().wait_send()
+            to_north().wait_recv()
+
+        @pl.when(has_north)
+        def _():
+            to_north().wait_send()
+            to_south().wait_recv()
+
     def aligned(i):
         return pl.multiple_of(i, SUB)
 
@@ -462,10 +466,17 @@
     def half_place(group):
         return pl.ds(half_at + group // 2 * SUB, SUB), pl.ds(group % 2 * (LANES // 2), LANES // 2)
 
-    def go_copy(part, target, source):
+    inner = (whole - 1) * 3 * chunk
+    piece = go.shape[2]
+
+    def slot(tile):
+        return ((tile + whole - 1) % whole) * 3 * chunk
+
+    def go_copy(part, target, source, side):
+        span = pl.ds(0, inner) if side == 0 else pl.ds(inner, piece - inner)
         return pltpu.make_async_remote_copy(
-            src_ref=go.at[target, part], dst_ref=recv.at[source, part],
-            send_sem=go_send.at[target, part], recv_sem=go_recv.at[source, part],
+            src_ref=go.at[target, part, span, :], dst_ref=recv.at[source, part, span, :],
+            send_sem=go_send.at[side, target, part], recv_sem=go_recv.at[side, source, part],
             device_id={"lon": target}, device_id_type=MESH,
         )
 
@@ -476,17 +487,18 @@
             device_id={"lon": target}, device_id_type=MESH,
         )
 
-    def make_piece(buf, place, part, target):
+    def make_piece(buf, place, part, target, inside=True, outside=True):
         first = (target * share + part * chunk) // SUB
         for i in range(per_chunk):
-            values = tendency_group(first + i)
+            values = tendency_group(first + i, edges=outside)
             for c in range(3):
                 group = c * per_chunk + i
                 for t in range(whole):
-                    buf[place, part, t * 3 * chunk + group * SUB : t * 3 * chunk + (group + 1) * SUB, :] = (
-                        values[c][:, t * LANES : (t + 1) * LANES]
-                    )
-                if cols % LANES:
+                    if outside if t == 0 else inside:
+                        buf[place, part, slot(t) + group * SUB : slot(t) + (group + 1) * SUB, :] = (
+                            values[c][:, t * LANES : (t + 1) * LANES]
+                        )
+                if outside and cols % LANES:
                     at_rows, at_lanes = half_place(group)
                     buf[place, part, at_rows, at_lanes] = values[c][:, whole * LANES :]
 
@@ -495,7 +507,7 @@
         for c in range(3):
             for t in range(whole):
                 out_ref[c, pl.ds(aligned(first), chunk), t * LANES : (t + 1) * LANES] = buf[
-                    source, part, pl.ds((t * 3 + c) * chunk, chunk), :
+                    source, part, pl.ds(slot(t) + c * chunk, chunk), :
                 ]
             if cols % LANES:
                 for i in range(per_chunk):
@@ -504,15 +516,39 @@
                         source, part, at_rows, at_lanes
                     ]
 
+    def nth(i):
+        return lax.rem(i + 1, chunks)
+
     @pl.when(polar)
     def _():
-        @pl.loop(0, chunks)
-        def _(part):
+        @pl.loop(1, lon_count)
+        def _(k):
+            target = lax.rem(lon + k, lon_count)
+            make_piece(go, target, nth(0), target, outside=False)
+            go_copy(nth(0), target, lon, 0).start()
+
+    halos_arrive()
+
+    @pl.when(polar)
+    def _():
+        @pl.loop(1, lon_count)
+        def _(k):
+            target = lax.rem(lon + k, lon_count)
+            make_piece(go, target, nth(0), target, inside=False)
+            go_copy(nth(0), target, lon, 1).start()
+
+        make_piece(recv, lon, nth(0), lon)
+
+        @pl.loop(1, chunks)
+        def _(i):
+            part = nth(i)
+
             @pl.loop(1, lon_count)
             def _(k):
                 target = lax.rem(lon + k, lon_count)
                 make_piece(go, target, part, target)
-                go_copy(part, target, lon).start()
+                go_copy(part, target, lon, 0).start()
+                go_copy(part, target, lon, 1).start()
 
             make_piece(recv, lon, part, lon)
 
@@ -532,13 +568,15 @@
     @pl.when(polar)
     def _():
         @pl.loop(0, chunks)
-        def _(part):
+        def _(i):
+            part = nth(i)
             for k in range(1, lon_count):
-                go_copy(part, lon, lax.rem(lon + k, lon_count)).wait_recv()
+                for side in range(2):
+                    go_copy(part, lon, lax.rem(lon + k, lon_count), side).wait_recv()
             for d in range(lon_count):
                 for t in range(whole):
                     lanes = slice(d * cols + t * LANES, d * cols + (t + 1) * LANES)
-                    full[:, lanes] = recv[d, part, t * 3 * chunk : (t + 1) * 3 * chunk, :]
+                    full[:, lanes] = recv[d, part, slot(t) : slot(t) + 3 * chunk, :]
                 if cols % LANES:
                     lanes = slice(d * cols + whole * LANES, (d + 1) * cols)
                     for group in range(3 * per_chunk):
@@ -557,7 +595,7 @@
 
             wanted = cut_start + part * chunk + lax.broadcasted_iota(jnp.int32, (chunk, 2 * rows), 0)
             hit = wanted == lax.broadcasted_iota(jnp.int32, (chunk, 2 * rows), 1)
-            cuts = cut_ref[0:1, :].astype(jnp.float32)
+            cuts = cut_ref[...].astype(jnp.float32)[None, :]
             limit = jnp.sum(jnp.where(hit, cuts, 0.0), axis=1, keepdims=True)
             limit = jnp.concatenate([limit, limit, limit], axis=0)
 
@@ -579,7 +617,7 @@
             for d in range(lon_count):
                 for t in range(whole):
                     lanes = slice(d * cols + t * LANES, d * cols + (t + 1) * LANES)
-                    ret[d, part, t * 3 * chunk : (t + 1) * 3 * chunk, :] = full[:, lanes]
+                    ret[d, part, slot(t) : slot(t) + 3 * chunk, :] = full[:, lanes]
                 if cols % LANES:
                     lanes = slice(d * cols + whole * LANES, (d + 1) * cols)
                     for group in range(3 * per_chunk):
@@ -590,11 +628,14 @@
             unpack(ret, part, lon)
 
         @pl.loop(0, chunks)
-        def _(part):
+        def _(i):
+            part = nth(i)
+
             @pl.loop(1, lon_count)
             def _(k):
                 other = lax.rem(lon + k, lon_count)
-                go_copy(part, other, lon).wait_send()
+                for side in range(2):
+                    go_copy(part, other, lon, side).wait_send()
                 back_copy(part, lon, other).wait_recv()
                 unpack(back, part, other)
                 back_copy(part, other, lon).wait_send()
@@ -613,7 +654,7 @@
     piece = (cols // LANES * groups + (groups + 1) // 2 * (cols % LANES > 0)) * SUB
     operands = [
         pltpu.with_memory_space_constraint(jnp.asarray(a), pltpu.HBM)
-        for a in (state_now, geo, polar_cutoff.reshape(1, 2 * rows), bins, fwd)
+        for a in (state_now, geo, polar_cutoff, bins, fwd)
     ]
     hbm_spec = pl.BlockSpec(memory_space=pltpu.HBM)
     vmem_spec = pl.BlockSpec(memory_space=pltpu.VMEM)
@@ -626,7 +667,7 @@
         scratch_shapes=[
             pltpu.VMEM((comps, rows + 2 * SUB, cols), jnp.float32),
             pltpu.VMEM((rows, LANES), jnp.float32),
-            pltpu.VMEM((1, 2 * rows), jnp.int32),
+            pltpu.VMEM((2 * rows,), jnp.int32),
             pltpu.VMEM((half, SUB, 2 * LANES), jnp.float32),
             pltpu.VMEM((lon_count, chunks, piece, LANES), jnp.float32),
             pltpu.VMEM((lon_count, chunks, piece, LANES), jnp.float32),
@@ -638,7 +679,7 @@
             pltpu.VMEM((2, comps, SUB, LANES), jnp.float32),
             pltpu.VMEM((2, comps, SUB, LANES), jnp.float32),
             dma, dma((4,)), dma((2,)), dma((2,)), dma((2,)), dma((2,)),
-            dma((lon_count, chunks)), dma((lon_count, chunks)),
+            dma((2, lon_count, chunks)), dma((2, lon_count, chunks)),
             dma((lon_count, chunks)), dma((lon_count, chunks)),
         ],
         compiler_params=pltpu.CompilerParams(
@@ -649,7 +690,7 @@
 
 
 def chunk_rows(share):
-    for parts in (3, 2, 4, 1):
+    for parts in (3, 4, 5):
         if share % (parts * SUB) == 0:
             return share // parts
     return 0
@@ -664,7 +705,7 @@
         share = rows // lon_count
         fits = (
             lat_count >= 4 and lat_total == 4 * rows and rows % lon_count == 0
-            and share % SUB == 0 and cols % (LANES // 2) == 0 and rows // SUB <= LANES
+            and chunk_rows(share) > 0 and cols % (LANES // 2) == 0 and cols >= 2 * LANES and rows // SUB <= LANES
             and lon_total % (2 * LANES) == 0 and comps == 3 * mesh.shape["ens"]
         )
         body = per_device

time: 58 us -> 53.3 us (0.919)
  Pallas kernels: 55 us -> 51.6 us
  local copies, waits for them, and re-layouts: 1.27 us -> 0.01 us
    pallas_call x1, Pallas kernels: 55 us -> 51.6 us  [fused_step(): pl.pallas_call(functools.partial(step_kernel, lat_count, lon_count, chunk...]
    reshape x1 -> x0, local copies, waits for them, and re-layouts: 1.27 us -> none  [fused_step(): polar_cutoff.reshape(1, 2 * rows)]
where the time goes in v2:
time: 53.3 us; the launch traced here: 53.2 us
  Pallas kernels  51.6 us (97%)
  other arithmetic  1.6 us (3%)
    pallas_call x1, Pallas kernels, fused_step(): pl.pallas_call(functools.partial(step_kernel, lat_count, lon_count, chunk...  51.6 us
    add x1, other arithmetic, fused_step(): return state_old + step_scale * filtered  1.6 us

profile of v2, /device:TPU:0, one launch (start us, length us, event | category | flops | bytes accessed | tf_op | source)
XLA Modules:
  0.0 53.2 jit_solution(17553183605669505135)
XLA Ops:
  0.0 0.0 copy-start
  0.0 51.6 %shard_map.64 = f32[3,288,576]{2,1,0:T(8,128)S(1)} custom-call(f32[3,288,576]{2,1,0:T(8,128)} %x_hbm.1, f32[1152,128]{1,0:T(8,128)} %constant.8.clone.geo_hbm, s32[576]{0:T(1024)} %cut_hbm.1, f32[9,8,256]{2,1,0:T(8,128)} %constant.9.clone.bins_hbm, bf16[2,9,256,256]{3,2,1,0:T(8,128)(2,1)} %constant.10.clone.fwd_hbm), custom_call_target="tpu_custom_call" | custom-call | tf_op jit(solution)/shard_map/pallas_call | solution.py:662
  51.6 0.0 copy-done
  51.6 1.6 %multiply_add_fusion = f32[3,288,576]{2,1,0:T(8,128)} fusion(f32[3,288,576]{2,1,0:T(8,128)S(1)} %copy-done, f32[3,288,576]{2,1,0:T(8,128)S(1)} %shard_map.64), kind=kLoop, calls=%fused_computation | loop fusion | flops 995328 | bytes 5971968 | tf_op jit(solution)/shard_map/add | solution.py:689
Async XLA Ops:
  0.0 51.6 %copy-start = (f32[3,288,576]{2,1,0:T(8,128)S(1)}, f32[3,288,576]{2,1,0:T(8,128)}, u32[]{:S(2)}) copy-start(f32[3,288,576]{2,1,0:T(8,128)} %param.7) | copy-start | bytes 5971972

commit v3 on v2

--- a/solution.py
+++ b/solution.py
@@ -295,8 +295,8 @@
 
 def step_kernel(
     lat_count, lon_count, chunk,
-    x_hbm, geo_hbm, cut_hbm, bins_hbm, fwd_hbm, out_ref,
-    xp, geo, cut_ref, bins, go, recv, ret, back, full, spec, fwd, col_send, col_recv,
+    x_hbm, old_hbm, geo_hbm, cut_hbm, bins_hbm, fwd_hbm, out_ref,
+    old, xp, geo, cut_ref, bins, go, recv, ret, back, full, spec, fwd, col_send, col_recv,
     load_sem, table_sem, row_send_sem, row_recv_sem, col_send_sem, col_recv_sem,
     go_send, go_recv, back_send, back_recv,
 ):
@@ -322,7 +322,7 @@
     geo_load.start()
     table_loads = [
         pltpu.make_async_copy(src, dst, table_sem.at[i + 1])
-        for i, (src, dst) in enumerate([(fwd_hbm, fwd), (bins_hbm, bins), (cut_hbm, cut_ref)])
+        for i, (src, dst) in enumerate([(fwd_hbm, fwd), (bins_hbm, bins), (cut_hbm, cut_ref), (old_hbm, old)])
     ]
     for copy in table_loads:
         copy.start()
@@ -456,6 +456,17 @@
             to_north().wait_send()
             to_south().wait_recv()
 
+    near = (lon_count + 1) // 2
+    side_start = lon // near * near
+
+    def partner(k):
+        if lon_count % 2:
+            return lax.rem(lon + k, lon_count)
+        place = lon - side_start
+        across = near - side_start + lax.rem(place + k - 1, near)
+        beside = side_start + lax.rem(place + k - near, near)
+        return jnp.where(k <= near, across, beside)
+
     def aligned(i):
         return pl.multiple_of(i, SUB)
 
@@ -506,15 +517,14 @@
         first = source * share + part * chunk
         for c in range(3):
             for t in range(whole):
-                out_ref[c, pl.ds(aligned(first), chunk), t * LANES : (t + 1) * LANES] = buf[
-                    source, part, pl.ds(slot(t) + c * chunk, chunk), :
-                ]
+                at = (c, pl.ds(aligned(first), chunk), slice(t * LANES, (t + 1) * LANES))
+                value = buf[source, part, pl.ds(slot(t) + c * chunk, chunk), :]
+                out_ref[at] = old[at] + step_scale * value
             if cols % LANES:
                 for i in range(per_chunk):
                     at_rows, at_lanes = half_place(c * per_chunk + i)
-                    out_ref[c, pl.ds(aligned(first + i * SUB), SUB), whole * LANES :] = buf[
-                        source, part, at_rows, at_lanes
-                    ]
+                    at = (c, pl.ds(aligned(first + i * SUB), SUB), slice(whole * LANES, cols))
+                    out_ref[at] = old[at] + step_scale * buf[source, part, at_rows, at_lanes]
 
     def nth(i):
         return lax.rem(i + 1, chunks)
@@ -523,7 +533,7 @@
     def _():
         @pl.loop(1, lon_count)
         def _(k):
-            target = lax.rem(lon + k, lon_count)
+            target = partner(k)
             make_piece(go, target, nth(0), target, outside=False)
             go_copy(nth(0), target, lon, 0).start()
 
@@ -533,7 +543,7 @@
     def _():
         @pl.loop(1, lon_count)
         def _(k):
-            target = lax.rem(lon + k, lon_count)
+            target = partner(k)
             make_piece(go, target, nth(0), target, inside=False)
             go_copy(nth(0), target, lon, 1).start()
 
@@ -545,12 +555,15 @@
 
             @pl.loop(1, lon_count)
             def _(k):
-                target = lax.rem(lon + k, lon_count)
+                target = partner(k)
                 make_piece(go, target, part, target)
                 go_copy(part, target, lon, 0).start()
                 go_copy(part, target, lon, 1).start()
 
             make_piece(recv, lon, part, lon)
+
+    for copy in table_loads:
+        copy.wait()
 
     @pl.when(jnp.logical_not(polar))
     def _():
@@ -558,10 +571,8 @@
         def _(g):
             values = tendency_group(g)
             for c in range(3):
-                out_ref[c, pl.ds(aligned(g * SUB), SUB), :] = values[c]
-
-    for copy in table_loads:
-        copy.wait()
+                at = (c, pl.ds(aligned(g * SUB), SUB), slice(None))
+                out_ref[at] = old[at] + step_scale * values[c]
 
     cut_start = jnp.where(lat == 0, 0, rows) + lon * share
 
@@ -572,7 +583,7 @@
             part = nth(i)
             for k in range(1, lon_count):
                 for side in range(2):
-                    go_copy(part, lon, lax.rem(lon + k, lon_count), side).wait_recv()
+                    go_copy(part, lon, partner(k), side).wait_recv()
             for d in range(lon_count):
                 for t in range(whole):
                     lanes = slice(d * cols + t * LANES, d * cols + (t + 1) * LANES)
@@ -624,7 +635,7 @@
                         at_rows, at_lanes = half_place(group)
                         ret[d, part, at_rows, at_lanes] = full[group * SUB : (group + 1) * SUB, lanes]
             for k in range(1, lon_count):
-                back_copy(part, lax.rem(lon + k, lon_count), lon).start()
+                back_copy(part, partner(k), lon).start()
             unpack(ret, part, lon)
 
         @pl.loop(0, chunks)
@@ -633,7 +644,7 @@
 
             @pl.loop(1, lon_count)
             def _(k):
-                other = lax.rem(lon + k, lon_count)
+                other = partner(k)
                 for side in range(2):
                     go_copy(part, other, lon, side).wait_send()
                 back_copy(part, lon, other).wait_recv()
@@ -654,7 +665,7 @@
     piece = (cols // LANES * groups + (groups + 1) // 2 * (cols % LANES > 0)) * SUB
     operands = [
         pltpu.with_memory_space_constraint(jnp.asarray(a), pltpu.HBM)
-        for a in (state_now, geo, polar_cutoff, bins, fwd)
+        for a in (state_now, state_old, geo, polar_cutoff, bins, fwd)
     ]
     hbm_spec = pl.BlockSpec(memory_space=pltpu.HBM)
     vmem_spec = pl.BlockSpec(memory_space=pltpu.VMEM)
@@ -662,9 +673,10 @@
     filtered = pl.pallas_call(
         functools.partial(step_kernel, lat_count, lon_count, chunk),
         out_shape=jax.ShapeDtypeStruct(state_now.shape, jnp.float32),
-        in_specs=[hbm_spec] * 5,
+        in_specs=[hbm_spec] * 6,
         out_specs=vmem_spec,
         scratch_shapes=[
+            pltpu.VMEM((comps, rows, cols), jnp.float32),
             pltpu.VMEM((comps, rows + 2 * SUB, cols), jnp.float32),
             pltpu.VMEM((rows, LANES), jnp.float32),
             pltpu.VMEM((2 * rows,), jnp.int32),
@@ -678,7 +690,7 @@
             pltpu.VMEM((2, half, 2 * LANES, 2 * LANES), jnp.bfloat16),
             pltpu.VMEM((2, comps, SUB, LANES), jnp.float32),
             pltpu.VMEM((2, comps, SUB, LANES), jnp.float32),
-            dma, dma((4,)), dma((2,)), dma((2,)), dma((2,)), dma((2,)),
+            dma, dma((5,)), dma((2,)), dma((2,)), dma((2,)), dma((2,)),
             dma((2, lon_count, chunks)), dma((2, lon_count, chunks)),
             dma((lon_count, chunks)), dma((lon_count, chunks)),
         ],
@@ -686,7 +698,7 @@
             collective_id=0, has_side_effects=True, vmem_limit_bytes=48 * 1024 * 1024
         ),
     )(*operands)
-    return state_old + step_scale * filtered
+    return filtered
 
 
 def chunk_rows(share):

time: 53.3 us -> 53 us (level)
  other arithmetic: 1.6 us -> 0 us
  local copies, waits for them, and re-layouts: 0.01 us -> 1.36 us
    add x1 -> x0, other arithmetic: 1.6 us -> none  [fused_step(): return state_old + step_scale * filtered]
    unnamed x2 -> x1, local copies, waits for them, and re-layouts: 0.01 us -> 1.36 us
where the time goes in v3:
time: 53 us; the launch traced here: 52.8 us
  Pallas kernels  51.5 us (97%)
  local copies, waits for them, and re-layouts  1.36 us (3%)
    pallas_call x1, Pallas kernels, fused_step(): pl.pallas_call(functools.partial(step_kernel, lat_count, lon_count, chunk...  51.5 us
    unnamed x1, local copies, waits for them, and re-layouts  1.36 us

profile of v3, /device:TPU:0, one launch (start us, length us, event | category | flops | bytes accessed | tf_op | source)
XLA Modules:
  0.0 52.8 jit_solution(1259739473396898169)
XLA Ops:
  0.0 51.5 %shard_map.64 = f32[3,288,576]{2,1,0:T(8,128)S(1)} custom-call(f32[3,288,576]{2,1,0:T(8,128)} %x_hbm.1, f32[3,288,576]{2,1,0:T(8,128)} %old_hbm.1, f32[1152,128]{1,0:T(8,128)} %constant.6.clone.geo_hbm, s32[576]{0:T(1024)} %cut_hbm.1, f32[9,8,256]{2,1,0:T(8,128)} %constant.7.clone.bins_hbm, bf16[2,9,256,256]{3,2,1,0:T(8,128)(2,1)} %constant.8.clone.fwd_hbm), custom_call_target="tpu_custom_call" | custom-call | tf_op jit(solution)/shard_map/pallas_call | solution.py:673
  51.5 1.4 %copy.8 = f32[3,288,576]{2,1,0:T(8,128)} copy(f32[3,288,576]{2,1,0:T(8,128)S(1)} %shard_map.64) | data formatting | bytes 3981312
